TPU v7x, 32 devices: a whole 2x2x4 slice. The times are simulated.
32 devices in a mesh: dp: 16 (over z, y, core), mp: 2 (over x).
Axes of the slice: x: 2, y: 2, z: 4, core: 2. Of those that a mesh axis runs over, the one named last changes fastest.
Arguments:
- tokens: bfloat16 [2048, 2048], P('dp', 'mp'), may hold values from -32 to 32
- lengths: int32 [4], replicated, may hold values from 1 to 1536, 2048 in all
- keep_mask: int32 [2048], replicated, may hold values 0 or 1
- routes: int32 [2048, 8], P('dp'), may hold values from 0 to 63, all different within a row; in each aligned block of 128 rows (0 to 127, 128 to 255, ...) at most 32 rows name the same one
- attention_gain: float32 [2048], replicated, may hold values from 0.1 to 1.9
- mixture_gain: float32 [2048], P('mp'), may hold values from 0.1 to 1.9
- query_gain: float32 [128], replicated, may hold values from 0.5 to 8, as said below
- key_gain: float32 [128], replicated, may hold values from 0.5 to 8, as said below
- query_weight: bfloat16 [2048, 2048], P('dp', 'mp'), may hold values from -0.125 to 0.125
- key_weight: bfloat16 [2048, 2048], P('dp', 'mp'), may hold values from -0.125 to 0.125
- value_weight: bfloat16 [2048, 2048], P('dp', 'mp'), may hold values from -0.125 to 0.125
- output_weight: bfloat16 [2048, 2048], P('mp', 'dp'), may hold values from -0.1875 to 0.1875
- router_weight: float32 [2048, 64], P('mp'), may hold values from -0.125 to 0.125
- expert_gate: bfloat16 [16, 2048, 4096], P('dp', None, 'mp'), may hold values from -0.125 to 0.125
- expert_up: bfloat16 [16, 2048, 4096], P('dp', None, 'mp'), may hold values from -0.125 to 0.125
- expert_down: bfloat16 [16, 4096, 2048], P('dp', 'mp'), may hold values from -0.25 to 0.25
Outputs:
- layer_output: bfloat16 [2048, 2048], P('dp', 'mp')
Inputs may be any that keep to these rules, and one draw needn't show every extreme that they name: The lengths sum to 2048; exactly one is 1536. `routes`: each row names 8 different experts. Within each aligned block of 128 rows (the rows of one index of dp) no expert is named by more than 32 rows, a bound that some block reaches. `query_gain`: Positive. `key_gain`: Positive.
All inputs are finite; a program needn't handle non-finite values.
Results may differ from a plain program's by a relative error of at most 0.012.
The roundings to bfloat16 on the way count: a program that leaves them out, or rounds other values in their place, can miss the bound.
Values may be sent and summed in bfloat16 or wider, within the bound.
A program may use at most 128 MiB of HBM per device.

v0:
```python
import jax
import jax.numpy as jnp
from jax import lax
from jax.sharding import PartitionSpec as P

D = 2048
HEAD_DIM = 128
FF = 1024
EXPERTS = 64
TOPK = 8
CAP = 32
EPS = 1e-06
ROPE_BASE = 10000.0
NEG = -1e30


def rope_tables(position):
    halves = HEAD_DIM // 2
    exponent = jnp.arange(halves, dtype=jnp.float32) * (2.0 / HEAD_DIM)
    frequency = jnp.power(jnp.float32(ROPE_BASE), -exponent)
    angle = position.astype(jnp.float32)[:, None] * frequency[None, :]
    cos_table = jnp.cos(angle)
    sin_table = jnp.sin(angle)
    return (jnp.concatenate([cos_table, cos_table], 1), jnp.concatenate([sin_table, sin_table], 1))


def head_prep(projected, head_gain, cos_table, sin_table):
    row_count = projected.shape[0]
    per_head = projected.reshape(row_count, -1, HEAD_DIM)
    normed = (
        per_head * lax.rsqrt(jnp.mean(per_head * per_head, axis=2, keepdims=True) + EPS) * head_gain
    )
    halves = HEAD_DIM // 2
    rotated = jnp.concatenate([-normed[:, :, halves:], normed[:, :, :halves]], 2)
    turned = normed * cos_table[:, None, :] + rotated * sin_table[:, None, :]
    return turned.reshape(row_count, -1).astype(jnp.bfloat16)


def segment_info(lengths, first_row, row_count):
    request_end = jnp.cumsum(lengths)
    request_start = request_end - lengths
    global_row = first_row + jnp.arange(row_count, dtype=jnp.int32)
    segment = jnp.sum((request_end[None, :] <= global_row[:, None]).astype(jnp.int32), axis=1)
    chosen = segment[:, None] == jnp.arange(lengths.shape[0], dtype=jnp.int32)[None, :]
    begin = jnp.sum(jnp.where(chosen, request_start[None, :], 0), axis=1)
    return (segment, global_row - begin, global_row)


def local(
    tokens,
    lengths,
    keep_mask,
    routes,
    attention_gain,
    mixture_gain,
    query_gain,
    key_gain,
    query_weight,
    key_weight,
    value_weight,
    output_weight,
    router_weight,
    expert_gate,
    expert_up,
    expert_down,
):
    tok_rows = tokens.shape[0]
    dp_count = lax.axis_size("dp")
    first_row = lax.axis_index("dp") * tok_rows
    full_tokens = lax.all_gather(tokens, "mp", axis=1, tiled=True)
    xfloat = full_tokens.astype(jnp.float32)
    normed_in = (
        xfloat * lax.rsqrt(jnp.mean(xfloat * xfloat, axis=1, keepdims=True) + EPS) * attention_gain
    ).astype(jnp.bfloat16)
    segment, position, global_row = segment_info(lengths, first_row, tok_rows)
    cos_table, sin_table = rope_tables(position)
    local_width = query_weight.shape[1]
    query_proj = jnp.dot(
        normed_in,
        lax.all_gather(query_weight, "dp", axis=0, tiled=True),
        preferred_element_type=jnp.float32,
    )
    key_proj = jnp.dot(
        normed_in,
        lax.all_gather(key_weight, "dp", axis=0, tiled=True),
        preferred_element_type=jnp.float32,
    )
    value_proj = jnp.dot(
        normed_in,
        lax.all_gather(value_weight, "dp", axis=0, tiled=True),
        preferred_element_type=jnp.float32,
    )
    queries = head_prep(query_proj, query_gain, cos_table, sin_table)
    key_heads = head_prep(key_proj, key_gain, cos_table, sin_table)
    value_heads = value_proj.astype(jnp.bfloat16)
    local_heads = local_width // HEAD_DIM
    query_split = queries.reshape(tok_rows, local_heads, HEAD_DIM)
    seg_low = segment[0]
    seg_high = segment[tok_rows - 1]
    scale = HEAD_DIM ** (-0.5)
    start_state = (
        jnp.full((local_heads, tok_rows), NEG, jnp.float32),
        jnp.zeros((local_heads, tok_rows), jnp.float32),
        jnp.zeros((tok_rows, local_heads, HEAD_DIM), jnp.float32),
    )
    key_piece = lax.all_gather(key_heads, "dp", axis=0, tiled=True)
    value_piece = lax.all_gather(value_heads, "dp", axis=0, tiled=True)
    piece_rows = key_piece.shape[0]
    key_seg, unused_pos, key_row = segment_info(lengths, jnp.int32(0), piece_rows)

    def compute(state_now):
        run_max, run_sum, run_acc = state_now
        key_split = key_piece.reshape(piece_rows, local_heads, HEAD_DIM)
        value_split = value_piece.reshape(piece_rows, local_heads, HEAD_DIM)
        scores = (
            jnp.einsum("thd,shd->hts", query_split, key_split, preferred_element_type=jnp.float32)
            * scale
        )
        visible = (segment[:, None] == key_seg[None, :]) & (
            (keep_mask[None, :] == 1) | (global_row[:, None] == key_row[None, :])
        )
        masked = jnp.where(visible[None], scores, NEG)
        new_max = jnp.maximum(run_max, jnp.max(masked, axis=2))
        factor = jnp.exp(run_max - new_max)
        weights = jnp.where(visible[None], jnp.exp(masked - new_max[:, :, None]), 0.0)
        new_sum = jnp.sum(weights, axis=2)
        mixed = jnp.einsum(
            "hts,shd->thd",
            weights.astype(jnp.bfloat16),
            value_split,
            preferred_element_type=jnp.float32,
        )
        new_acc = run_acc * factor.T[:, :, None] + mixed
        return (new_max, new_sum, new_acc)

    touches = (key_seg[piece_rows - 1] >= seg_low) & (key_seg[0] <= seg_high)
    final_max, final_sum, final_acc = lax.cond(
        touches, compute, lambda state_now: state_now, start_state
    )
    attended = (
        (final_acc / final_sum.T[:, :, None]).reshape(tok_rows, local_width).astype(jnp.bfloat16)
    )
    partial_out = jnp.dot(
        attended,
        lax.all_gather(output_weight, "dp", axis=1, tiled=True),
        preferred_element_type=jnp.float32,
    )
    summed_out = lax.psum_scatter(partial_out, "mp", scatter_dimension=1, tiled=True)
    residual = (tokens.astype(jnp.float32) + summed_out).astype(jnp.bfloat16)
    hfloat = residual.astype(jnp.float32)
    scaled = hfloat * mixture_gain
    partial_logits = jnp.dot(scaled, router_weight, precision=lax.Precision.HIGHEST)
    square_sum, logit_sum = lax.psum((jnp.sum(hfloat * hfloat, axis=1), partial_logits), "mp")
    inverse = lax.rsqrt(square_sum / D + EPS)[:, None]
    mixed_in = (scaled * inverse).astype(jnp.bfloat16)
    logits = logit_sum * inverse
    picked = jnp.take_along_axis(logits, routes, axis=1)
    sigmoid_vals = jax.nn.sigmoid(picked)
    route_weight = sigmoid_vals / jnp.sum(sigmoid_vals, axis=1, keepdims=True)
    onehot = jnp.sum(
        (routes[:, :, None] == jnp.arange(EXPERTS, dtype=jnp.int32)[None, None, :]).astype(
            jnp.int32
        ),
        axis=1,
    )
    before = jnp.cumsum(onehot, axis=0) - onehot
    slot = jnp.take_along_axis(before, routes, axis=1)
    target = routes * CAP + slot
    token_ids = jnp.repeat(jnp.arange(tok_rows, dtype=jnp.int32), TOPK)
    source = jnp.full((EXPERTS * CAP,), tok_rows, jnp.int32).at[target.reshape(-1)].set(token_ids)
    exp_local = EXPERTS // dp_count
    gate_local = expert_gate[0]
    up_local = expert_up[0]
    down_local = expert_down[0]
    unit_count = gate_local.shape[1]
    mp_index = lax.axis_index("mp")
    full_in = lax.all_gather(mixed_in, "mp", axis=1, tiled=True)
    padded = jnp.concatenate([full_in, jnp.zeros((1, full_in.shape[1]), jnp.bfloat16)], 0)
    sending = padded[source].reshape(dp_count, exp_local, CAP, full_in.shape[1])
    rows_in = lax.all_to_all(sending, "dp", split_axis=0, concat_axis=0, tiled=True)
    if unit_count <= FF:
        owners = FF // unit_count
        expert_index = mp_index // owners
        own_rows = lax.dynamic_index_in_dim(rows_in, expert_index, 1, keepdims=False)
        gate_val = jnp.einsum(
            "scd,dh->sch", own_rows, gate_local, preferred_element_type=jnp.float32
        )
        up_val = jnp.einsum("scd,dh->sch", own_rows, up_local, preferred_element_type=jnp.float32)
        hidden = (jax.nn.silu(gate_val) * up_val).astype(jnp.bfloat16)
        own_part = jnp.einsum("sch,hd->scd", hidden, down_local, preferred_element_type=jnp.float32)
        selector = (jnp.arange(exp_local, dtype=jnp.int32) == expert_index).astype(jnp.float32)
        partial_rows = own_part[:, None, :, :] * selector[None, :, None, None]
    else:
        held = unit_count // FF
        first_expert = mp_index * held
        own_rows = lax.dynamic_slice_in_dim(rows_in, first_expert, held, 1)
        gate_val = jnp.einsum(
            "secd,def->secf",
            own_rows,
            gate_local.reshape(gate_local.shape[0], held, FF),
            preferred_element_type=jnp.float32,
        )
        up_val = jnp.einsum(
            "secd,def->secf",
            own_rows,
            up_local.reshape(up_local.shape[0], held, FF),
            preferred_element_type=jnp.float32,
        )
        hidden = (jax.nn.silu(gate_val) * up_val).astype(jnp.bfloat16)
        own_part = jnp.einsum(
            "secf,efd->secd",
            hidden,
            down_local.reshape(held, FF, down_local.shape[1]),
            preferred_element_type=jnp.float32,
        )
        empty_rows = jnp.zeros(
            (rows_in.shape[0], exp_local, rows_in.shape[2], own_part.shape[3]), jnp.float32
        )
        partial_rows = lax.dynamic_update_slice_in_dim(empty_rows, own_part, first_expert, 1)
    summed_rows = lax.psum_scatter(
        partial_rows.astype(jnp.bfloat16), "mp", scatter_dimension=3, tiled=True
    )
    returned = lax.all_to_all(summed_rows, "dp", split_axis=0, concat_axis=0, tiled=True)
    flat = returned.reshape(EXPERTS * CAP, local_width)
    gathered = flat[target]
    mixture = jnp.sum(gathered.astype(jnp.float32) * route_weight[:, :, None], axis=1)
    return (hfloat + mixture).astype(jnp.bfloat16)


def solution(mesh):
    return jax.shard_map(
        local,
        mesh=mesh,
        in_specs=(
            P("dp", "mp"),
            P(),
            P(),
            P("dp", None),
            P(),
            P("mp"),
            P(),
            P(),
            P("dp", "mp"),
            P("dp", "mp"),
            P("dp", "mp"),
            P("mp", "dp"),
            P("mp", None),
            P("dp", None, "mp"),
            P("dp", None, "mp"),
            P("dp", "mp", None),
        ),
        out_specs=P("dp", "mp"),
        check_vma=False,
    )
```

profile of v0, /device:TPU:13, one launch (start us, length us, event | category | flops | bytes accessed | tf_op | source)
XLA Modules:
  0.0 811.3 jit_solution(14257861319533035457)
XLA Ops:
  10.9 8.1 all_gather.24
  19.9 41.0 %all-gather.9.cloned.1.call-done = bf16[2048,1024]{1,0:T(8,128)(2,1)} async-done(((bf16[128,1024]{1,0:T(8,128)(2,1)}), bf16[2048,1024]{1,0:T(8,128)(2,1)}) %all-gather.9.cloned.1.call-update) | async-done | bytes 4194320 | tf_op jit(solution)/shard_map/all_gather | solution.py:85
  64.4 47.8 %all-gather.7.cloned.1.call-done = bf16[2048,1024]{1,0:T(8,128)(2,1)} async-done(((bf16[128,1024]{1,0:T(8,128)(2,1)}), bf16[2048,1024]{1,0:T(8,128)(2,1)}) %all-gather.7.cloned.1.call-update) | async-done | bytes 4194320 | tf_op jit(solution)/shard_map/all_gather | solution.py:80
  118.6 44.8 %all-gather.13.cloned.1.call-done = bf16[2048,1024]{1,0:T(8,128)(2,1)} async-done(((bf16[128,1024]{1,0:T(8,128)(2,1)}), bf16[2048,1024]{1,0:T(8,128)(2,1)}) %all-gather.13.cloned.1.call-update) | async-done | bytes 4194320 | tf_op jit(solution)/shard_map/all_gather | solution.py:90
  163.4 3.6 convolution_convert_fusion
  171.0 43.5 %all-gather.11.cloned.1.call-done = bf16[2048,1024]{1,0:T(8,128)(2,1)} async-done(((bf16[128,1024]{1,0:T(8,128)(2,1)}), bf16[2048,1024]{1,0:T(8,128)(2,1)}) %all-gather.11.cloned.1.call-update) | async-done | bytes 4194320 | tf_op jit(solution)/shard_map/all_gather | solution.py:106
  214.5 51.1 %all-gather.15.cloned.1.call-done = bf16[2048,1024]{1,0:T(8,128)(2,1)} async-done(((bf16[128,1024]{1,0:T(8,128)(2,1)}), bf16[2048,1024]{1,0:T(8,128)(2,1)}) %all-gather.15.cloned.1.call-update) | async-done | bytes 4194320 | tf_op jit(solution)/shard_map/all_gather | solution.py:107
  265.6 16.5 %conditional.1 = (f32[8,128]{1,0:T(8,128)S(1)}, f32[128,8,128]{0,2,1:T(8,128)S(1)}) conditional(s32[]{:T(128)} %bitcast.4, () %tuple.13, (s32[128]{0:T(128)S(1)}, s32[2048]{0:T(1024)S(1)}, s32[2048]{0:T(1024)S(1)}, s32[]{:T(128)}, s32[128]{0:T(128)S(1)}, /*index=5*/s32[2048]{0:T(1024)S(1)}, bf16[128,1024]{1,0:T(8,128)(2,1)S(1)}, ...), branch_computations={%region_7.8_spmd, %region_8.11_spmd} | conditional | flops 1102187648 | bytes 86833224 | solution.py:137
  266.0 4.6 fusion
  270.6 3.2 copy-done.2
  273.8 3.3 fusion.19
  277.3 4.7 fusion.2
  282.1 35.4 %all-gather.17.cloned.1.call-done = bf16[1024,2048]{1,0:T(8,128)(2,1)} async-done(((bf16[1024,128]{1,0:T(8,128)(2,1)}), bf16[1024,2048]{1,0:T(8,128)(2,1)}) %all-gather.17.cloned.1.call-update) | async-done | bytes 4194320 | tf_op jit(solution)/shard_map/all_gather | solution.py:145
  317.5 3.9 fusion.73
  322.0 7.1 gather_fusion.2
  329.6 4.3 scatter_custom_fusion
  334.0 8.4 %reduce-scatter.3.cloned.1.call-done = f32[128,1024]{1,0:T(8,128)} async-done(((f32[128,2048]{1,0:T(8,128)}), f32[128,1024]{1,0:T(8,128)}) %reduce-scatter.3.cloned.1.call-update) | async-done | bytes 524304 | tf_op jit(solution)/shard_map/reduce_scatter | solution.py:148
  344.3 5.5 all-reduce.1
  349.9 5.9 all_gather.31
  355.9 11.0 %gather_fusion = bf16[2048,2048]{1,0:T(8,128)(2,1)} fusion(bf16[129,2048]{1,0:T(8,128)(2,1)S(1)} %concatenate.19, s32[2048]{0:T(1024)S(1)} %fusion.62), kind=kCustom, calls=%fused_computation | custom fusion | bytes 16785408 | tf_op jit(solution)/shard_map/gather | solution.py:179
  366.9 9.5 %all-to-all-start = ((bf16[16,4,32,2048]{3,2,1,0:T(8,128)(2,1)}), bf16[16,4,32,2048]{3,2,1,0:T(8,128)(2,1)}, u32[]{:S(2)}, u32[]{:S(2)}) async-start(bf16[16,4,32,2048]{3,2,1,0:T(8,128)(2,1)} %bitcast.130), calls=%async_computation.1 | async-start | bytes 16777216 | tf_op jit(solution)/shard_map/all_to_all | solution.py:180
  376.5 14.4 %reshape_squeeze.10 = bf16[2048,2,1024]{2,1,0:T(2,128)(2,1)} reshape(bf16[1,2048,2048]{2,1,0:T(8,128)(2,1)} %param.32) | data formatting | bytes 16777216 | tf_op jit(solution)/shard_map/reshape;squeeze | solution.py:206
  390.9 14.5 %reshape_squeeze.9 = bf16[2048,2,1024]{2,1,0:T(2,128)(2,1)} reshape(bf16[1,2048,2048]{2,1,0:T(8,128)(2,1)} %param.31) | data formatting | bytes 16777216 | tf_op jit(solution)/shard_map/reshape;squeeze | solution.py:200
  405.4 153.3 %all-to-all-done = bf16[16,4,32,2048]{3,2,1,0:T(8,128)(2,1)} async-done(((bf16[16,4,32,2048]{3,2,1,0:T(8,128)(2,1)}), bf16[16,4,32,2048]{3,2,1,0:T(8,128)(2,1)}, u32[]{:S(2)}, u32[]{:S(2)}) %all-to-all-start) | async-done | bytes 8388640 | tf_op jit(solution)/shard_map/all_to_all | solution.py:180
  558.8 11.3 %fusion.29 = f32[2,16,32,1024]{3,2,1,0:T(8,128)} fusion(bf16[2048,2,1024,1]{2,1,0,3:T(2,128)(2,1)} %bitcast.132, bf16[16,4,32,2048]{3,2,1,0:T(8,128)(2,1)} %all-to-all-done, s32[]{:T(128)S(6)} %select_n.52), kind=kOutput, calls=%fused_computation.32 | convolution fusion | flops 4294967296 | bytes 16777220 | tf_op jit(solution)/shard_map/secd,def->secf/dot_general | solution.py:203
  570.0 20.3 %convolution_bitcast_fusion = bf16[16,2,32,2048]{3,2,0,1:T(8,128)(2,1)} fusion(bf16[2,1024,2048,1]{2,1,3,0:T(8,128)(2,1)} %bitcast.147, f32[2,16,32,1024]{3,2,1,0:T(8,128)} %fusion.29, bf16[2048,2,1024,1]{2,1,0,3:T(2,128)(2,1)} %bitcast.131, bf16[16,4,32,2048]{3,2,1,0:T(8,128)(2,1)} %all-to-all-done, s32[]{:T(128)S(6)} %select_n.52), kind=kOutput, calls=%fused_computation.37 | convolution fusion | flops 8596226048 | bytes 29360132 | tf_op jit(solution)/shard_map/secf,efd->secd/dot_general | solution.py:210
  590.3 4.3 broadcast_in_dim.70
  596.9 98.9 %reduce-scatter.5.cloned.1.call-done = bf16[16,4,32,1024]{3,2,1,0:T(8,128)(2,1)} async-done(((bf16[16,4,32,2048]{3,2,1,0:T(8,128)(2,1)}), bf16[16,4,32,1024]{3,2,1,0:T(8,128)(2,1)}) %reduce-scatter.5.cloned.1.call-update) | async-done | bytes 4194320 | tf_op jit(solution)/shard_map/reduce_scatter | solution.py:220
  695.8 6.3 all-to-all-start.1
  702.4 7.0 gather_fusion.3
  709.7 84.9 %all-to-all-done.1 = bf16[16,4,32,1024]{3,2,1,0:T(8,128)(2,1)} async-done(((bf16[16,4,32,1024]{3,2,1,0:T(8,128)(2,1)}), bf16[16,4,32,1024]{3,2,1,0:T(8,128)(2,1)}, u32[]{:S(2)}, u32[]{:S(2)}) %all-to-all-start.1) | async-done | bytes 4194336 | tf_op jit(solution)/shard_map/all_to_all | solution.py:223
  794.6 7.7 gather_fusion.1
  (114 shorter events, 24.8 us)
Async XLA Ops:
  6.5 337.1 %copy-start = (f32[1024,64]{0,1:T(8,128)S(1)}, f32[1024,64]{0,1:T(8,128)}, u32[]{:S(2)}) copy-start(f32[1024,64]{0,1:T(8,128)} %param.30) | copy-start | bytes 786436
  6.5 54.4 %all-gather.9.cloned.1.call-start = ((), (), s32[]{:S(2)}) async-start(), calls=%async_computation.5 | async-start | bytes 4456448 | tf_op jit(solution)/shard_map/all_gather | solution.py:85
  7.3 104.9 %all-gather.7.cloned.1.call-start = ((), (), s32[]{:S(2)}) async-start(), calls=%async_computation.4 | async-start | bytes 4456448 | tf_op jit(solution)/shard_map/all_gather | solution.py:80
  8.0 155.4 %all-gather.13.cloned.1.call-start = ((), (), s32[]{:S(2)}) async-start(), calls=%async_computation.7 | async-start | bytes 4456448 | tf_op jit(solution)/shard_map/all_gather | solution.py:90
  8.7 205.8 %all-gather.11.cloned.1.call-start = ((), (), s32[]{:S(2)}) async-start(), calls=%async_computation.6 | async-start | bytes 4456448 | tf_op jit(solution)/shard_map/all_gather | solution.py:106
  10.9 101.2 %copy-start.6 = (f32[2048]{0:T(1024)S(1)}, f32[2048]{0:T(1024)}, u32[]{:S(2)}) copy-start(f32[2048]{0:T(1024)} %param.22) | copy-start | bytes 24580
  63.9 51.7 %copy-start.9 = (f32[128]{0:T(128)S(1)}, f32[128]{0:T(128)}, u32[]{:S(2)}) copy-start(f32[128]{0:T(128)} %param.25) | copy-start | bytes 1540
  64.2 51.6 %copy-start.10 = (f32[128]{0:T(128)S(1)}, f32[128]{0:T(128)}, u32[]{:S(2)}) copy-start(f32[128]{0:T(128)} %param.24) | copy-start | bytes 1540
  117.2 148.4 %copy-start.8 = (s32[2048]{0:T(1024)S(1)}, s32[2048]{0:T(1024)}, u32[]{:S(2)}) copy-start(s32[2048]{0:T(1024)} %param.20) | copy-start | bytes 24580
  118.5 147.1 %all-gather.15.cloned.1.call-start = ((), (), s32[]{:S(2)}) async-start(), calls=%async_computation.8 | async-start | bytes 4456448 | tf_op jit(solution)/shard_map/all_gather | solution.py:107
  167.1 150.5 %all-gather.17.cloned.1.call-start = ((), (), s32[]{:S(2)}) async-start(), calls=%async_computation.9 | async-start | bytes 4456448 | tf_op jit(solution)/shard_map/all_gather | solution.py:145
  167.7 174.8 %reduce-scatter.3.cloned.1.call-start = ((), (), s32[]{:S(2)}) async-start(), calls=%async_computation.10 | async-start | bytes 1572864 | tf_op jit(solution)/shard_map/reduce_scatter | solution.py:148
  266.0 7.8 copy-start.11
  270.6 3.2 copy-start.2
  282.1 39.4 %copy-start.5 = (s32[128,8]{0,1:T(8,128)S(1)}, s32[128,8]{0,1:T(8,128)}, u32[]{:S(2)}) copy-start(s32[128,8]{0,1:T(8,128)} %param.21) | copy-start | bytes 12292
  322.0 20.4 %copy-start.4 = (bf16[128,1024]{1,0:T(8,128)(2,1)S(1)}, bf16[128,1024]{1,0:T(8,128)(2,1)}, u32[]{:S(2)}) copy-start(bf16[128,1024]{1,0:T(8,128)(2,1)} %param.18) | copy-start | bytes 786436
  322.0 21.6 %copy-start.7 = (f32[1024]{0:T(1024)S(1)}, f32[1024]{0:T(1024)}, u32[]{:S(2)}) copy-start(f32[1024]{0:T(1024)} %param.23) | copy-start | bytes 12292
  366.9 191.9 %all-to-all-start = ((bf16[16,4,32,2048]{3,2,1,0:T(8,128)(2,1)}), bf16[16,4,32,2048]{3,2,1,0:T(8,128)(2,1)}, u32[]{:S(2)}, u32[]{:S(2)}) async-start(bf16[16,4,32,2048]{3,2,1,0:T(8,128)(2,1)} %bitcast.130), calls=%async_computation.1 | async-start | bytes 16777216 | tf_op jit(solution)/shard_map/all_to_all | solution.py:180
  376.4 319.4 %reduce-scatter.5.cloned.1.call-start = ((), (), s32[]{:S(2)}) async-start(), calls=%async_computation.11 | async-start | bytes 12582912 | tf_op jit(solution)/shard_map/reduce_scatter | solution.py:220
  590.3 4.3 copy-start.3
  695.8 98.8 %all-to-all-start.1 = ((bf16[16,4,32,1024]{3,2,1,0:T(8,128)(2,1)}), bf16[16,4,32,1024]{3,2,1,0:T(8,128)(2,1)}, u32[]{:S(2)}, u32[]{:S(2)}) async-start(bf16[16,4,32,1024]{3,2,1,0:T(8,128)(2,1)} %reduce-scatter.5.cloned.1.call-done), calls=%async_computation.3 | async-start | bytes 8388608 | tf_op jit(solution)/shard_map/all_to_all | solution.py:223
  794.6 9.8 %copy-start.1 = (f32[1024,64]{0,1:T(8,128)S(1)}, f32[1024,64]{0,1:T(8,128)}, u32[]{:S(2)}) copy-start(f32[1024,64]{0,1:T(8,128)} %param.30) | copy-start | bytes 786436
Sparse Core Ops, SparseCore 0:
  9.5 51.3 all-gather.8
  63.1 49.0 all-gather.6
  114.3 49.0 all-gather.12
  165.4 49.0 all-gather.10
  216.5 49.0 all-gather.14
  267.6 49.8 all-gather.16
  321.6 20.7 reduce-scatter.2
  597.0 98.7 reduce-scatter.4
where the time goes:
time: 813 us; the launch traced here: 811 us
  waiting for transfers between devices  612 us (75%)
  local copies, waits for them, and re-layouts  79.6 us (10%)
  matrix products  53.6 us (7%)
  blocking collectives  19.5 us (2%)
  between operations  16.5 us (2%)
  starting transfers between devices  16.2 us (2%)
  other arithmetic  14 us (2%)
    all_to_all x1, waiting for transfers between devices, local(): lax.all_to_all(sending, 'dp', split_axis=0, concat_axis=0, tiled=True)  153 us
    reduce_scatter x1, waiting for transfers between devices, local(): lax.psum_scatter(partial_rows.astype(jnp.bfloat16), 'mp', scatter_dimensi...  98.9 us
    all_to_all x1, waiting for transfers between devices, local(): lax.all_to_all(summed_rows, 'dp', split_axis=0, concat_axis=0, tiled=True)  84.9 us
    all_gather x1, waiting for transfers between devices, local(): value_piece = lax.all_gather(value_heads, 'dp', axis=0, tiled=True)  51.1 us
    all_gather x1, waiting for transfers between devices, local(): lax.all_gather(query_weight, 'dp', axis=0, tiled=True)  47.8 us
    all_gather x1, waiting for transfers between devices, local(): lax.all_gather(value_weight, 'dp', axis=0, tiled=True)  44.8 us
    all_gather x1, waiting for transfers between devices, local(): key_piece = lax.all_gather(key_heads, 'dp', axis=0, tiled=True)  43.5 us
    all_gather x1, waiting for transfers between devices, local(): lax.all_gather(key_weight, 'dp', axis=0, tiled=True)  41 us
  transfers between devices with their start and end apart: 10, of which 10 were waited for; matrix products, arithmetic and copies ran while one was open for 10% of the time, Pallas kernels for 0%

commit v1 on v0

--- a/solution.py
+++ b/solution.py
@@ -12,6 +12,15 @@
 EPS = 1e-06
 ROPE_BASE = 10000.0
 NEG = -1e30
+
+
+def _spread_panels(slab_in, frame, which_axis):
+    out_arr = jnp.split(
+        lax.all_gather(jnp.concatenate([slab_in, frame], 1), which_axis, tiled=True, axis=0),
+        [slab_in.shape[1]],
+        1,
+    )
+    return out_arr
 
 
 def rope_tables(position):
@@ -103,8 +112,7 @@
         jnp.zeros((local_heads, tok_rows), jnp.float32),
         jnp.zeros((tok_rows, local_heads, HEAD_DIM), jnp.float32),
     )
-    key_piece = lax.all_gather(key_heads, "dp", axis=0, tiled=True)
-    value_piece = lax.all_gather(value_heads, "dp", axis=0, tiled=True)
+    key_piece, value_piece = _spread_panels(key_heads, value_heads, "dp")
     piece_rows = key_piece.shape[0]
     key_seg, unused_pos, key_row = segment_info(lengths, jnp.int32(0), piece_rows)
 

time: 813 us -> 788 us (0.969)
  waiting for transfers between devices: 612 us -> 574 us
  local copies, waits for them, and re-layouts: 79.6 us -> 95.9 us
    all_gather x2 -> x1, waiting for transfers between devices: 94.6 us -> 69.1 us  [_spread_panels(): lax.all_gather(jnp.concatenate([slab_in, frame], 1), which_axis, tiled=Tr...]
    all_gather x1, waiting for transfers between devices: 35.4 us -> 22.3 us  [local(): lax.all_gather(output_weight, 'dp', axis=1, tiled=True)]
    another operation x0 -> x1, local copies, waits for them, and re-layouts: none -> 12.4 us
  transfers between devices with their start and end apart: 10 -> 9, of which waited for: 10 -> 9; matrix products, arithmetic and copies ran while one was open for 10% -> 11% of each run, Pallas kernels for 0% -> 0%
where the time goes in v1:
time: 788 us; the launch traced here: 786 us
  waiting for transfers between devices  574 us (73%)
  local copies, waits for them, and re-layouts  95.9 us (12%)
  matrix products  50.1 us (6%)
  blocking collectives  19.5 us (2%)
  between operations  16.4 us (2%)
  starting transfers between devices  16.1 us (2%)
  other arithmetic  14.4 us (2%)
    all_to_all x1, waiting for transfers between devices, local(): lax.all_to_all(sending, 'dp', split_axis=0, concat_axis=0, tiled=True)  153 us
    reduce_scatter x1, waiting for transfers between devices, local(): lax.psum_scatter(partial_rows.astype(jnp.bfloat16), 'mp', scatter_dimensi...  98.8 us
    all_to_all x1, waiting for transfers between devices, local(): lax.all_to_all(summed_rows, 'dp', split_axis=0, concat_axis=0, tiled=True)  84.9 us
    all_gather x1, waiting for transfers between devices, _spread_panels(): lax.all_gather(jnp.concatenate([slab_in, frame], 1), which_axis, tiled=Tr...  69.1 us
    all_gather x1, waiting for transfers between devices, local(): lax.all_gather(query_weight, 'dp', axis=0, tiled=True)  47.8 us
    all_gather x1, waiting for transfers between devices, local(): lax.all_gather(value_weight, 'dp', axis=0, tiled=True)  45.4 us
    all_gather x1, waiting for transfers between devices, local(): lax.all_gather(key_weight, 'dp', axis=0, tiled=True)  41 us
    all_gather x1, waiting for transfers between devices, local(): lax.all_gather(output_weight, 'dp', axis=1, tiled=True)  22.3 us
  transfers between devices with their start and end apart: 9, of which 9 were waited for; matrix products, arithmetic and copies ran while one was open for 11% of the time, Pallas kernels for 0%

profile of v1, /device:TPU:13, one launch (start us, length us, event | category | flops | bytes accessed | tf_op | source)
XLA Modules:
  0.0 786.3 jit_solution(17624591800150043721)
XLA Ops:
  10.9 8.1 %all_gather.21 = bf16[128,2048]{1,0:T(8,128)(2,1)S(1)} all-gather(bf16[128,1024]{1,0:T(8,128)(2,1)} %param.18), channel_id=1, replica_groups=mesh['dp'=16,'mp'=2] {'mp'}, dimensions={1}, use_global_device_ids=true | all-gather | bytes 786432 | tf_op jit(solution)/shard_map/all_gather | solution.py:79
  19.9 41.0 %all-gather.8.cloned.1.call-done = bf16[2048,1024]{1,0:T(8,128)(2,1)} async-done(((bf16[128,1024]{1,0:T(8,128)(2,1)}), bf16[2048,1024]{1,0:T(8,128)(2,1)}) %all-gather.8.cloned.1.call-update) | async-done | bytes 4194320 | tf_op jit(solution)/shard_map/all_gather | solution.py:94
  60.9 3.0 fusion.56
  64.4 47.8 %all-gather.6.cloned.1.call-done = bf16[2048,1024]{1,0:T(8,128)(2,1)} async-done(((bf16[128,1024]{1,0:T(8,128)(2,1)}), bf16[2048,1024]{1,0:T(8,128)(2,1)}) %all-gather.6.cloned.1.call-update) | async-done | bytes 4194320 | tf_op jit(solution)/shard_map/all_gather | solution.py:89
  118.0 45.4 %all-gather.10.cloned.1.call-done = bf16[2048,1024]{1,0:T(8,128)(2,1)} async-done(((bf16[128,1024]{1,0:T(8,128)(2,1)}), bf16[2048,1024]{1,0:T(8,128)(2,1)}) %all-gather.10.cloned.1.call-update) | async-done | bytes 4194320 | tf_op jit(solution)/shard_map/all_gather | solution.py:99
  163.4 2.9 convolution_convert_fusion
  171.1 69.1 %all-gather.12.cloned.1.call-done = bf16[2048,2048]{1,0:T(8,128)(2,1)} async-done(((bf16[128,2048]{1,0:T(8,128)(2,1)}), bf16[2048,2048]{1,0:T(8,128)(2,1)}) %all-gather.12.cloned.1.call-update) | async-done | bytes 8388624 | tf_op jit(solution)/shard_map/all_gather | solution.py:19
  240.2 30.0 %conditional.1 = (f32[8,128]{1,0:T(8,128)S(1)}, f32[128,8,128]{0,2,1:T(8,128)S(1)}) conditional(s32[]{:T(128)} %bitcast.6, () %tuple.13, (s32[128]{0:T(128)S(1)}, s32[2048]{0:T(1024)S(1)}, s32[2048]{0:T(1024)S(1)}, s32[]{:T(128)}, s32[128]{0:T(128)S(1)}, /*index=5*/s32[2048]{0:T(1024)S(1)}, bf16[128,1024]{1,0:T(8,128)(2,1)S(1)}, ...), branch_computations={%region_7.8_spmd, %region_8.11_spmd} | conditional | flops 1102187648 | bytes 103610416 | solution.py:145
  240.6 12.4 %copy.100 = bf16[2048,2048]{0,1:T(8,128)(2,1)} copy(bf16[2048,2048]{1,0:T(8,128)(2,1)} %get-tuple-element.80) | data formatting | bytes 16777216 | tf_op jit(solution)/shard_map
  253.0 3.9 fusion.60
  259.1 3.2 copy-done.2
  265.5 4.7 fusion.2
  270.2 22.3 %all-gather.14.cloned.1.call-done = bf16[1024,2048]{1,0:T(8,128)(2,1)} async-done(((bf16[1024,128]{1,0:T(8,128)(2,1)}), bf16[1024,2048]{1,0:T(8,128)(2,1)}) %all-gather.14.cloned.1.call-update) | async-done | bytes 4194320 | tf_op jit(solution)/shard_map/all_gather | solution.py:153
  292.5 3.9 fusion.63
  297.0 7.1 gather_fusion.2
  304.6 4.3 scatter_custom_fusion
  308.9 8.4 %reduce-scatter.3.cloned.1.call-done = f32[128,1024]{1,0:T(8,128)} async-done(((f32[128,2048]{1,0:T(8,128)}), f32[128,1024]{1,0:T(8,128)}) %reduce-scatter.3.cloned.1.call-update) | async-done | bytes 524304 | tf_op jit(solution)/shard_map/reduce_scatter | solution.py:156
  319.3 5.5 all-reduce.1
  324.9 5.9 all_gather.27
  330.9 11.0 %gather_fusion = bf16[2048,2048]{1,0:T(8,128)(2,1)} fusion(bf16[129,2048]{1,0:T(8,128)(2,1)S(1)} %concatenate.23, s32[2048]{0:T(1024)S(1)} %fusion.51), kind=kCustom, calls=%fused_computation | custom fusion | bytes 16785408 | tf_op jit(solution)/shard_map/gather | solution.py:187
  341.9 9.5 %all-to-all-start = ((bf16[16,4,32,2048]{3,2,1,0:T(8,128)(2,1)}), bf16[16,4,32,2048]{3,2,1,0:T(8,128)(2,1)}, u32[]{:S(2)}, u32[]{:S(2)}) async-start(bf16[16,4,32,2048]{3,2,1,0:T(8,128)(2,1)} %bitcast.114), calls=%async_computation.1 | async-start | bytes 16777216 | tf_op jit(solution)/shard_map/all_to_all | solution.py:188
  351.5 14.4 %reshape_squeeze.10 = bf16[2048,2,1024]{2,1,0:T(2,128)(2,1)} reshape(bf16[1,2048,2048]{2,1,0:T(8,128)(2,1)} %param.32) | data formatting | bytes 16777216 | tf_op jit(solution)/shard_map/reshape;squeeze | solution.py:214
  365.9 14.5 %reshape_squeeze.9 = bf16[2048,2,1024]{2,1,0:T(2,128)(2,1)} reshape(bf16[1,2048,2048]{2,1,0:T(8,128)(2,1)} %param.31) | data formatting | bytes 16777216 | tf_op jit(solution)/shard_map/reshape;squeeze | solution.py:208
  380.4 153.4 %all-to-all-done = bf16[16,4,32,2048]{3,2,1,0:T(8,128)(2,1)} async-done(((bf16[16,4,32,2048]{3,2,1,0:T(8,128)(2,1)}), bf16[16,4,32,2048]{3,2,1,0:T(8,128)(2,1)}, u32[]{:S(2)}, u32[]{:S(2)}) %all-to-all-start) | async-done | bytes 8388640 | tf_op jit(solution)/shard_map/all_to_all | solution.py:188
  533.8 11.3 %fusion.18 = f32[2,16,32,1024]{3,2,1,0:T(8,128)} fusion(bf16[2048,2,1024,1]{2,1,0,3:T(2,128)(2,1)} %bitcast.117, bf16[16,4,32,2048]{3,2,1,0:T(8,128)(2,1)} %all-to-all-done, s32[]{:T(128)S(6)} %select_n.52), kind=kOutput, calls=%fused_computation.25 | convolution fusion | flops 4294967296 | bytes 16777220 | tf_op jit(solution)/shard_map/secd,def->secf/dot_general | solution.py:211
  545.1 20.3 %convolution_bitcast_fusion = bf16[16,2,32,2048]{3,2,0,1:T(8,128)(2,1)} fusion(bf16[2,1024,2048,1]{2,1,3,0:T(8,128)(2,1)} %bitcast.133, f32[2,16,32,1024]{3,2,1,0:T(8,128)} %fusion.18, bf16[2048,2,1024,1]{2,1,0,3:T(2,128)(2,1)} %bitcast.116, bf16[16,4,32,2048]{3,2,1,0:T(8,128)(2,1)} %all-to-all-done, s32[]{:T(128)S(6)} %select_n.52), kind=kOutput, calls=%fused_computation.30 | convolution fusion | flops 8596226048 | bytes 29360132 | tf_op jit(solution)/shard_map/secf,efd->secd/dot_general | solution.py:218
  565.3 4.3 broadcast_in_dim.70
  571.9 98.8 %reduce-scatter.5.cloned.1.call-done = bf16[16,4,32,1024]{3,2,1,0:T(8,128)(2,1)} async-done(((bf16[16,4,32,2048]{3,2,1,0:T(8,128)(2,1)}), bf16[16,4,32,1024]{3,2,1,0:T(8,128)(2,1)}) %reduce-scatter.5.cloned.1.call-update) | async-done | bytes 4194320 | tf_op jit(solution)/shard_map/reduce_scatter | solution.py:228
  670.8 6.4 all-to-all-start.1
  677.4 7.0 gather_fusion.3
  684.7 84.9 %all-to-all-done.1 = bf16[16,4,32,1024]{3,2,1,0:T(8,128)(2,1)} async-done(((bf16[16,4,32,1024]{3,2,1,0:T(8,128)(2,1)}), bf16[16,4,32,1024]{3,2,1,0:T(8,128)(2,1)}, u32[]{:S(2)}, u32[]{:S(2)}) %all-to-all-start.1) | async-done | bytes 4194336 | tf_op jit(solution)/shard_map/all_to_all | solution.py:231
  769.6 7.7 gather_fusion.1
  (112 shorter events, 27.4 us)
Async XLA Ops:
  6.5 312.1 %copy-start = (f32[1024,64]{0,1:T(8,128)S(1)}, f32[1024,64]{0,1:T(8,128)}, u32[]{:S(2)}) copy-start(f32[1024,64]{0,1:T(8,128)} %param.30) | copy-start | bytes 786436
  6.5 54.4 %all-gather.8.cloned.1.call-start = ((), (), s32[]{:S(2)}) async-start(), calls=%async_computation.5 | async-start | bytes 4456448 | tf_op jit(solution)/shard_map/all_gather | solution.py:94
  7.3 104.9 %all-gather.6.cloned.1.call-start = ((), (), s32[]{:S(2)}) async-start(), calls=%async_computation.4 | async-start | bytes 4456448 | tf_op jit(solution)/shard_map/all_gather | solution.py:89
  8.0 155.4 %all-gather.10.cloned.1.call-start = ((), (), s32[]{:S(2)}) async-start(), calls=%async_computation.6 | async-start | bytes 4456448 | tf_op jit(solution)/shard_map/all_gather | solution.py:99
  8.7 231.5 %all-gather.12.cloned.1.call-start = ((), (), s32[]{:S(2)}) async-start(), calls=%async_computation.7 | async-start | bytes 8912896 | tf_op jit(solution)/shard_map/all_gather | solution.py:19
  10.9 101.2 %copy-start.6 = (f32[2048]{0:T(1024)S(1)}, f32[2048]{0:T(1024)}, u32[]{:S(2)}) copy-start(f32[2048]{0:T(1024)} %param.22) | copy-start | bytes 24580
  63.9 51.7 %copy-start.9 = (f32[128]{0:T(128)S(1)}, f32[128]{0:T(128)}, u32[]{:S(2)}) copy-start(f32[128]{0:T(128)} %param.25) | copy-start | bytes 1540
  64.2 51.6 %copy-start.10 = (f32[128]{0:T(128)S(1)}, f32[128]{0:T(128)}, u32[]{:S(2)}) copy-start(f32[128]{0:T(128)} %param.24) | copy-start | bytes 1540
  118.0 122.2 %copy-start.8 = (s32[2048]{0:T(1024)S(1)}, s32[2048]{0:T(1024)}, u32[]{:S(2)}) copy-start(s32[2048]{0:T(1024)} %param.20) | copy-start | bytes 24580
  167.3 125.2 %all-gather.14.cloned.1.call-start = ((), (), s32[]{:S(2)}) async-start(), calls=%async_computation.8 | async-start | bytes 4456448 | tf_op jit(solution)/shard_map/all_gather | solution.py:153
  167.9 149.5 %reduce-scatter.3.cloned.1.call-start = ((), (), s32[]{:S(2)}) async-start(), calls=%async_computation.9 | async-start | bytes 1572864 | tf_op jit(solution)/shard_map/reduce_scatter | solution.py:156
  259.1 3.2 copy-start.2
  270.2 26.3 %copy-start.5 = (s32[128,8]{0,1:T(8,128)S(1)}, s32[128,8]{0,1:T(8,128)}, u32[]{:S(2)}) copy-start(s32[128,8]{0,1:T(8,128)} %param.21) | copy-start | bytes 12292
  297.0 20.4 %copy-start.4 = (bf16[128,1024]{1,0:T(8,128)(2,1)S(1)}, bf16[128,1024]{1,0:T(8,128)(2,1)}, u32[]{:S(2)}) copy-start(bf16[128,1024]{1,0:T(8,128)(2,1)} %param.18) | copy-start | bytes 786436
  297.0 21.6 %copy-start.7 = (f32[1024]{0:T(1024)S(1)}, f32[1024]{0:T(1024)}, u32[]{:S(2)}) copy-start(f32[1024]{0:T(1024)} %param.23) | copy-start | bytes 12292
  341.9 191.9 %all-to-all-start = ((bf16[16,4,32,2048]{3,2,1,0:T(8,128)(2,1)}), bf16[16,4,32,2048]{3,2,1,0:T(8,128)(2,1)}, u32[]{:S(2)}, u32[]{:S(2)}) async-start(bf16[16,4,32,2048]{3,2,1,0:T(8,128)(2,1)} %bitcast.114), calls=%async_computation.1 | async-start | bytes 16777216 | tf_op jit(solution)/shard_map/all_to_all | solution.py:188
  351.4 319.3 %reduce-scatter.5.cloned.1.call-start = ((), (), s32[]{:S(2)}) async-start(), calls=%async_computation.10 | async-start | bytes 12582912 | tf_op jit(solution)/shard_map/reduce_scatter | solution.py:228
  565.3 4.3 copy-start.3
  670.8 98.8 %all-to-all-start.1 = ((bf16[16,4,32,1024]{3,2,1,0:T(8,128)(2,1)}), bf16[16,4,32,1024]{3,2,1,0:T(8,128)(2,1)}, u32[]{:S(2)}, u32[]{:S(2)}) async-start(bf16[16,4,32,1024]{3,2,1,0:T(8,128)(2,1)} %reduce-scatter.5.cloned.1.call-done), calls=%async_computation.3 | async-start | bytes 8388608 | tf_op jit(solution)/shard_map/all_to_all | solution.py:231
  769.6 9.8 %copy-start.1 = (f32[1024,64]{0,1:T(8,128)S(1)}, f32[1024,64]{0,1:T(8,128)}, u32[]{:S(2)}) copy-start(f32[1024,64]{0,1:T(8,128)} %param.30) | copy-start | bytes 786436
Sparse Core Ops, SparseCore 0:
  9.5 51.3 all-gather.7
  63.1 49.0 all-gather.5
  114.3 49.0 all-gather.9
  167.4 72.7 all-gather.11
  242.2 50.2 all-gather.13
  296.6 20.7 reduce-scatter.2
  572.1 98.6 reduce-scatter.4
